TPU v7x, 256 devices: a whole 4x4x8 slice. The times are simulated.
256 devices in a mesh: pipe: 4 (over x), dom: 64 (over y, z, core).
Axes of the slice: x: 4, y: 4, z: 8, core: 2. Of those that a mesh axis runs over, the one named last changes fastest.
Arguments:
- node_states: bfloat16 [4, 1, 4096, 512], P('pipe', None, 'dom'), may hold values from -6 to 6
- edge_states: bfloat16 [4, 1, 16384, 512], P('pipe', None, 'dom'), may hold values from -6 to 6
- node_cot: bfloat16 [1, 4096, 512], P(None, 'dom'), may hold values from -6 to 6
- edge_cot: bfloat16 [1, 16384, 512], P(None, 'dom'), may hold values from -6 to 6
- edge_w1: bfloat16 [4, 1536, 512], P('pipe'), may hold values from -0.15625 to 0.15625
- edge_w2: bfloat16 [4, 512, 512], P('pipe'), may hold values from -0.25 to 0.25
- edge_gain: bfloat16 [4, 512], P('pipe'), may hold values from 0.5 to 1.5
- node_w1: bfloat16 [4, 1024, 512], P('pipe'), may hold values from -0.1875 to 0.1875
- node_w2: bfloat16 [4, 512, 512], P('pipe'), may hold values from -0.25 to 0.25
- node_gain: bfloat16 [4, 512], P('pipe'), may hold values from 0.5 to 1.5
- edge_src: int32 [16384], P('dom'), may hold values from 0 to 191, as said below
- edge_dst: int32 [16384], P('dom'), may hold values from 0 to 63
- edge_count: int32 [64], P('dom'), may hold values from 128 to 256, as said below
- send_rows: int32 [64, 64, 2], P('dom'), may hold values from 0 to 63
Outputs:
- node_grads: bfloat16 [4, 1, 4096, 512], P('pipe', None, 'dom')
- edge_grads: bfloat16 [4, 1, 16384, 512], P('pipe', None, 'dom')
- edge_w1_grad: float32 [4, 1536, 512], P('pipe', 'dom')
- edge_w2_grad: float32 [4, 512, 512], P('pipe', 'dom')
- edge_gain_grad: float32 [4, 512], P('pipe', 'dom')
- node_w1_grad: float32 [4, 1024, 512], P('pipe', 'dom')
- node_w2_grad: float32 [4, 512, 512], P('pipe', 'dom')
- node_gain_grad: float32 [4, 512], P('pipe', 'dom')
Inputs may be any that keep to these rules, and one draw needn't show every extreme that they name: `edge_src`: each partition's edges name its own nodes below 64 and its received rows from 64 on; every received row is the sender of some live edge of its partition. `edge_count`: some partition has all 256 edges live in every draw.
All inputs are finite; a program needn't handle non-finite values.
Results may differ from a plain program's by a relative error of at most 0.04.
Values may be sent and summed in bfloat16 or wider, within the bound.
A program may use at most 64 MiB of HBM per device.

v0:
```python
import jax
import jax.numpy as jnp
from jax import lax
from jax.sharding import PartitionSpec as P

EPS = 1e-05


def passed_along(value, axis, steps):
    count = lax.axis_size(axis)
    first, last = (max(0, -steps), min(count, count - steps))
    return lax.ppermute(value, axis, [(source, source + steps) for source in range(first, last)])


def contract(former, latter):
    return lax.dot_general(
        former, latter, (((0,), (0,)), ((), ())), preferred_element_type=jnp.float32
    )


def mlp_forward(inputs, inner_weight, outer_weight):
    hidden_pre = jnp.dot(inputs, inner_weight, preferred_element_type=jnp.float32)
    hidden_act = jax.nn.silu(hidden_pre).astype(jnp.bfloat16)
    output = jnp.dot(hidden_act, outer_weight, preferred_element_type=jnp.float32)
    centred = output - jnp.mean(output, axis=-1, keepdims=True)
    rescale = lax.rsqrt(jnp.mean(centred * centred, axis=-1, keepdims=True) + EPS)
    return (hidden_pre, hidden_act, centred * rescale, rescale)


def mlp_backward(inner_weight, outer_weight, gain_vector, stored, cotangent):
    hidden_pre, hidden_act, normed, rescale = stored
    grad_norm = cotangent * gain_vector.astype(jnp.float32)
    grad_out = rescale * (
        grad_norm
        - jnp.mean(grad_norm, axis=-1, keepdims=True)
        - normed * jnp.mean(grad_norm * normed, axis=-1, keepdims=True)
    )
    grad_out = grad_out.astype(jnp.bfloat16)
    grad_act = jnp.dot(grad_out, outer_weight.T, preferred_element_type=jnp.float32)
    logistic = jax.nn.sigmoid(hidden_pre)
    grad_pre = (grad_act * logistic * (1.0 + hidden_pre * (1.0 - logistic))).astype(jnp.bfloat16)
    grad_in = jnp.dot(grad_pre, inner_weight.T, preferred_element_type=jnp.float32)
    return (grad_in, hidden_act, grad_out, grad_pre, jnp.sum(cotangent * normed, axis=0))


def layer_backward(
    node_rows, source_rows, edge_rows, receiver, live_mask, node_cotan, edge_cotan, params
):
    edge_inner, edge_outer, edge_scale, node_inner, node_outer, node_scale = params
    count_nodes = node_rows.shape[0]
    width = node_rows.shape[1]
    edge_input = jnp.concatenate([edge_rows, source_rows, node_rows[receiver]], axis=1)
    edge_stored = mlp_forward(edge_input, edge_inner, edge_outer)
    new_edges = edge_rows.astype(jnp.float32) + edge_stored[2] * edge_scale.astype(jnp.float32)
    aggregate = jax.ops.segment_sum(
        new_edges * live_mask[:, None], receiver, num_segments=count_nodes
    )
    node_input = jnp.concatenate([node_rows, aggregate.astype(jnp.bfloat16)], axis=1)
    node_stored = mlp_forward(node_input, node_inner, node_outer)
    node_back = mlp_backward(
        node_inner, node_outer, node_scale, node_stored, node_cotan.astype(jnp.float32)
    )
    node_grad_in = node_back[0]
    grad_edges = (edge_cotan.astype(jnp.float32) + node_grad_in[:, width:][receiver]) * live_mask[
        :, None
    ]
    edge_back = mlp_backward(edge_inner, edge_outer, edge_scale, edge_stored, grad_edges)
    edge_grad_in = edge_back[0]
    edge_result = (grad_edges + edge_grad_in[:, :width]).astype(jnp.bfloat16)
    node_partial = (
        node_cotan.astype(jnp.float32)
        + node_grad_in[:, :width]
        + jax.ops.segment_sum(edge_grad_in[:, 2 * width :], receiver, num_segments=count_nodes)
    )
    return (
        node_partial,
        edge_grad_in[:, width : 2 * width],
        edge_result,
        (edge_input,) + tuple(edge_back[1:]),
        (node_input,) + tuple(node_back[1:]),
    )


def weight_terms(edge_terms, node_terms):
    result = ()
    for terms in (edge_terms, node_terms):
        inputs, hidden_act, grad_out, grad_pre, gain_sum = terms
        result = result + (contract(inputs, grad_pre), contract(hidden_act, grad_out), gain_sum)
    return result


def pick_batch(array, index):
    return lax.dynamic_index_in_dim(array, index, 0, keepdims=False)


def on_device(
    node_states,
    edge_states,
    node_cot,
    edge_cot,
    edge_w1,
    edge_w2,
    edge_gain,
    node_w1,
    node_w2,
    node_gain,
    edge_src,
    edge_dst,
    edge_count,
    send_rows,
):
    phases = lax.axis_size("pipe")
    section = lax.axis_index("pipe")
    batches = node_states.shape[1]
    count_nodes = node_states.shape[2]
    count_edges = edge_states.shape[2]
    width = node_states.shape[3]
    params = (edge_w1[0], edge_w2[0], edge_gain[0], node_w1[0], node_w2[0], node_gain[0])
    live_mask = (jnp.arange(count_edges, dtype=jnp.int32) < edge_count[0]).astype(jnp.float32)
    outgoing = send_rows[0].reshape(-1)
    count_ghosts = outgoing.shape[0]
    is_top = section == phases - 1
    node_result = jnp.zeros((batches, count_nodes, width), jnp.bfloat16)
    edge_result = jnp.zeros((batches, count_edges, width), jnp.bfloat16)
    carried = jnp.zeros((count_nodes + count_edges, width), jnp.bfloat16)
    weight_sums = tuple((jnp.zeros(weight.shape, jnp.float32) for weight in params))
    for tick in range(batches + phases - 1):
        batch_index = tick - (phases - 1 - section)
        valid = jnp.logical_and(batch_index >= 0, batch_index < batches)
        slot_index = jnp.clip(batch_index, 0, batches - 1)
        if tick > 0:
            carried = passed_along(carried, "pipe", -1)
        node_cotan = jnp.where(is_top, pick_batch(node_cot, slot_index), carried[:count_nodes])
        edge_cotan = jnp.where(is_top, pick_batch(edge_cot, slot_index), carried[count_nodes:])
        node_rows = pick_batch(node_states[0], slot_index)
        edge_rows = pick_batch(edge_states[0], slot_index)
        ghosts = lax.all_to_all(node_rows[outgoing], "dom", split_axis=0, concat_axis=0, tiled=True)
        table = jnp.concatenate([node_rows, ghosts], axis=0)
        node_partial, source_grads, edge_out, edge_terms, node_terms = layer_backward(
            node_rows,
            table[edge_src],
            edge_rows,
            edge_dst,
            live_mask,
            node_cotan,
            edge_cotan,
            params,
        )
        source_sums = jax.ops.segment_sum(
            source_grads, edge_src, num_segments=count_nodes + count_ghosts
        )
        returned = lax.all_to_all(
            source_sums[count_nodes:].astype(jnp.bfloat16),
            "dom",
            split_axis=0,
            concat_axis=0,
            tiled=True,
        ).astype(jnp.float32)
        node_out = (
            node_partial
            + source_sums[:count_nodes]
            + jax.ops.segment_sum(returned, outgoing, num_segments=count_nodes)
        ).astype(jnp.bfloat16)
        carried = jnp.concatenate([node_out, edge_out], axis=0)
        node_result = node_result.at[slot_index].set(
            jnp.where(valid, node_out, pick_batch(node_result, slot_index))
        )
        edge_result = edge_result.at[slot_index].set(
            jnp.where(valid, edge_out, pick_batch(edge_result, slot_index))
        )
        valid_float = valid.astype(jnp.float32)
        terms = weight_terms(edge_terms, node_terms)
        weight_sums = tuple((total + valid_float * term for total, term in zip(weight_sums, terms)))
    reduced = lax.psum_scatter(weight_sums, "dom", scatter_dimension=0, tiled=True)
    return (
        node_result[None],
        edge_result[None],
        reduced[0][None],
        reduced[1][None],
        reduced[2][None],
        reduced[3][None],
        reduced[4][None],
        reduced[5][None],
    )


def solution(mesh):
    placed = (
        P("pipe", None, "dom", None),
        P("pipe", None, "dom", None),
        P(None, "dom", None),
        P(None, "dom", None),
        P("pipe", None, None),
        P("pipe", None, None),
        P("pipe", None),
        P("pipe", None, None),
        P("pipe", None, None),
        P("pipe", None),
        P("dom"),
        P("dom"),
        P("dom"),
        P("dom", None, None),
    )
    return jax.shard_map(
        on_device,
        mesh=mesh,
        in_specs=placed,
        out_specs=(
            P("pipe", None, "dom", None),
            P("pipe", None, "dom", None),
            P("pipe", "dom", None),
            P("pipe", "dom", None),
            P("pipe", "dom"),
            P("pipe", "dom", None),
            P("pipe", "dom", None),
            P("pipe", "dom"),
        ),
        check_vma=False,
    )
```

profile of v0, /device:TPU:32, one launch (start us, length us, event | category | flops | bytes accessed | tf_op | source)
XLA Modules:
  0.0 790.2 jit_solution(4240939096230444454)
XLA Ops:
  10.7 11.8 %all-to-all-start = ((bf16[64,2,512]{2,1,0:T(2,128)(2,1)}), bf16[64,2,512]{2,1,0:T(2,128)(2,1)S(1)}, u32[]{:S(2)}, u32[]{:S(2)}) async-start(bf16[64,2,512]{2,1,0:T(2,128)(2,1)} %all_to_all.38), calls=%async_computation | async-start | bytes 262144 | tf_op jit(solution)/shard_map/all_to_all | solution.py:137
  25.7 6.8 all-to-all-done
  37.2 2.7 scatter_custom_fusion
  53.5 3.4 scatter_custom_fusion.1
  58.5 5.8 all-to-all-start.1
  65.9 4.1 scatter_custom_fusion.2
  80.6 10.3 %collective-permute-done = bf16[320,512]{1,0:T(8,128)(2,1)S(1)} collective-permute-done((bf16[320,512]{1,0:T(8,128)(2,1)S(1)}, bf16[320,512]{1,0:T(8,128)(2,1)S(1)}, u32[]{:S(2)}, u32[]{:S(2)}) %collective-permute-start) | collective-permute-done | bytes 327712 | tf_op jit(solution)/shard_map/ppermute | solution.py:12
  104.4 3.4 scatter_custom_fusion.4
  111.1 8.3 %all-to-all-start.2 = ((bf16[64,2,512]{2,1,0:T(2,128)(2,1)}), bf16[64,2,512]{2,1,0:T(2,128)(2,1)}, u32[]{:S(2)}, u32[]{:S(2)}) async-start(bf16[64,2,512]{2,1,0:T(2,128)(2,1)} %all_to_all.43), calls=%async_computation.2 | async-start | bytes 262144 | tf_op jit(solution)/shard_map/all_to_all | solution.py:152
  121.0 4.1 scatter_custom_fusion.5
  139.9 8.0 %collective-permute-done.1 = bf16[320,512]{1,0:T(8,128)(2,1)} collective-permute-done((bf16[320,512]{1,0:T(8,128)(2,1)}, bf16[320,512]{1,0:T(8,128)(2,1)}, u32[]{:S(2)}, u32[]{:S(2)}) %collective-permute-start.1) | collective-permute-done | bytes 327712 | tf_op jit(solution)/shard_map/ppermute | solution.py:12
  161.1 3.4 scatter_custom_fusion.7
  167.7 8.3 %all-to-all-start.3 = ((bf16[64,2,512]{2,1,0:T(2,128)(2,1)}), bf16[64,2,512]{2,1,0:T(2,128)(2,1)}, u32[]{:S(2)}, u32[]{:S(2)}) async-start(bf16[64,2,512]{2,1,0:T(2,128)(2,1)} %all_to_all.45), calls=%async_computation.3 | async-start | bytes 262144 | tf_op jit(solution)/shard_map/all_to_all | solution.py:152
  177.7 4.1 scatter_custom_fusion.8
  196.5 7.2 collective-permute-done.2
  229.7 3.1 scatter_custom_fusion.10
  236.1 3.8 scatter_custom_fusion.11
  241.5 8.3 %all-to-all-start.4 = ((bf16[64,2,512]{2,1,0:T(2,128)(2,1)}), bf16[64,2,512]{2,1,0:T(2,128)(2,1)}, u32[]{:S(2)}, u32[]{:S(2)}) async-start(bf16[64,2,512]{2,1,0:T(2,128)(2,1)} %all_to_all.47), calls=%async_computation.4 | async-start | bytes 262144 | tf_op jit(solution)/shard_map/all_to_all | solution.py:152
  251.7 124.0 %all-reduce.2 = (f32[512]{0:T(512)S(1)}, f32[512]{0:T(512)S(1)}) all-reduce(f32[512]{0:T(512)} %multiply_add_fusion.4, f32[512]{0:T(512)} %multiply_add_fusion.3), channel_id=4, replica_groups=mesh['pipe'=4,'dom'=64] {'dom'}, use_global_device_ids=true, to_apply=%region_43.44.clone | all-reduce | flops 1024 | bytes 8192
  376.8 4.5 fusion.82
  383.8 4.2 fusion.125
  388.0 105.2 %reduce-scatter.11.cloned.1.call-done = f32[8,512]{1,0:T(8,128)} async-done(((f32[512,512]{1,0:T(8,128)}), f32[8,512]{1,0:T(8,128)}) %reduce-scatter.11.cloned.1.call-update) | async-done | bytes 16400 | tf_op jit(solution)/shard_map/reduce_scatter | solution.py:174
  493.2 144.5 %reduce-scatter.9.cloned.1.call-done = f32[16,512]{1,0:T(8,128)} async-done(((f32[1024,512]{1,0:T(8,128)}), f32[16,512]{1,0:T(8,128)}) %reduce-scatter.9.cloned.1.call-update) | async-done | bytes 32784 | tf_op jit(solution)/shard_map/reduce_scatter | solution.py:174
  637.7 145.7 %reduce-scatter.5.cloned.1.call-done = f32[24,512]{1,0:T(8,128)} async-done(((f32[1536,512]{1,0:T(8,128)}), f32[24,512]{1,0:T(8,128)}) %reduce-scatter.5.cloned.1.call-update) | async-done | bytes 49168 | tf_op jit(solution)/shard_map/reduce_scatter | solution.py:174
  (360 shorter events, 138.6 us)
Async XLA Ops:
  7.2 27.3 %copy-start = (bf16[1,1536,512]{2,1,0:T(8,128)(2,1)S(1)}, bf16[1,1536,512]{2,1,0:T(8,128)(2,1)}, u32[]{:S(2)}) copy-start(bf16[1,1536,512]{2,1,0:T(8,128)(2,1)} %param.34) | copy-start | bytes 4718596
  7.2 16.7 %copy-start.1 = (bf16[1,1,64,512]{3,2,1,0:T(8,128)(2,1)S(1)}, bf16[1,1,64,512]{3,2,1,0:T(8,128)(2,1)}, u32[]{:S(2)}) copy-start(bf16[1,1,64,512]{3,2,1,0:T(8,128)(2,1)} %param.30) | copy-start | bytes 196612
  7.2 16.7 %copy-start.82 = (bf16[1,512]{1,0:T(2,128)(2,1)S(1)}, bf16[1,512]{1,0:T(2,128)(2,1)}, u32[]{:S(2)}) copy-start(bf16[1,512]{1,0:T(2,128)(2,1)} %param.36) | copy-start | bytes 3076
  10.7 21.8 %all-to-all-start = ((bf16[64,2,512]{2,1,0:T(2,128)(2,1)}), bf16[64,2,512]{2,1,0:T(2,128)(2,1)S(1)}, u32[]{:S(2)}, u32[]{:S(2)}) async-start(bf16[64,2,512]{2,1,0:T(2,128)(2,1)} %all_to_all.38), calls=%async_computation | async-start | bytes 262144 | tf_op jit(solution)/shard_map/all_to_all | solution.py:137
  58.5 15.7 %all-to-all-start.1 = ((bf16[64,2,512]{2,1,0:T(2,128)(2,1)}), bf16[64,2,512]{2,1,0:T(2,128)(2,1)S(1)}, u32[]{:S(2)}, u32[]{:S(2)}) async-start(bf16[64,2,512]{2,1,0:T(2,128)(2,1)} %all_to_all.41), calls=%async_computation.1 | async-start | bytes 262144 | tf_op jit(solution)/shard_map/all_to_all | solution.py:152
  78.3 16.0 %copy-start.38 = (bf16[64,512]{1,0:T(8,128)(2,1)}, bf16[64,512]{1,0:T(8,128)(2,1)S(1)}, u32[]{:S(2)}) copy-start(bf16[64,512]{1,0:T(8,128)(2,1)S(1)} %add_convert_fusion.3) | copy-start | bytes 196612
  79.3 11.6 %collective-permute-start = (bf16[320,512]{1,0:T(8,128)(2,1)S(1)}, bf16[320,512]{1,0:T(8,128)(2,1)S(1)}, u32[]{:S(2)}, u32[]{:S(2)}) collective-permute-start(bf16[320,512]{1,0:T(8,128)(2,1)S(1)} %pad_maximum_fusion.1), channel_id=1, source_target_pairs={{64,0},{128,64},{192,128},{65,1},{129,65},{193,129},{66,2},{130,66... | collective-permute-start | bytes 983048 | tf_op jit(solution)/shard_map/ppermute | solution.py:12
  111.1 18.3 %all-to-all-start.2 = ((bf16[64,2,512]{2,1,0:T(2,128)(2,1)}), bf16[64,2,512]{2,1,0:T(2,128)(2,1)}, u32[]{:S(2)}, u32[]{:S(2)}) async-start(bf16[64,2,512]{2,1,0:T(2,128)(2,1)} %all_to_all.43), calls=%async_computation.2 | async-start | bytes 262144 | tf_op jit(solution)/shard_map/all_to_all | solution.py:152
  134.3 16.7 %copy-start.40 = (bf16[64,512]{1,0:T(8,128)(2,1)}, bf16[64,512]{1,0:T(8,128)(2,1)S(1)}, u32[]{:S(2)}) copy-start(bf16[64,512]{1,0:T(8,128)(2,1)S(1)} %add_convert_fusion.2) | copy-start | bytes 196612
  136.0 11.9 %collective-permute-start.1 = (bf16[320,512]{1,0:T(8,128)(2,1)}, bf16[320,512]{1,0:T(8,128)(2,1)}, u32[]{:S(2)}, u32[]{:S(2)}) collective-permute-start(bf16[320,512]{1,0:T(8,128)(2,1)} %pad_maximum_fusion.2), channel_id=1, source_target_pairs={{64,0},{128,64},{192,128},{65,1},{129,65},{193,129},{66,2},{130,66... | collective-permute-start | bytes 983048 | tf_op jit(solution)/shard_map/ppermute | solution.py:12
  167.7 18.3 %all-to-all-start.3 = ((bf16[64,2,512]{2,1,0:T(2,128)(2,1)}), bf16[64,2,512]{2,1,0:T(2,128)(2,1)}, u32[]{:S(2)}, u32[]{:S(2)}) async-start(bf16[64,2,512]{2,1,0:T(2,128)(2,1)} %all_to_all.45), calls=%async_computation.3 | async-start | bytes 262144 | tf_op jit(solution)/shard_map/all_to_all | solution.py:152
  176.0 212.0 %reduce-scatter.7.cloned.1.call-start = ((), (), s32[]{:S(2)}) async-start(), calls=%async_computation.10 | async-start | bytes 1064960 | tf_op jit(solution)/shard_map/reduce_scatter | solution.py:174
  192.1 11.6 %collective-permute-start.2 = (bf16[320,512]{1,0:T(8,128)(2,1)S(1)}, bf16[320,512]{1,0:T(8,128)(2,1)S(1)}, u32[]{:S(2)}, u32[]{:S(2)}) collective-permute-start(bf16[320,512]{1,0:T(8,128)(2,1)S(1)} %pad_maximum_fusion.3), channel_id=1, source_target_pairs={{64,0},{128,64},{192,128},{65,1},{129,65},{193,129},{66,2},{130,66... | collective-permute-start | bytes 983048 | tf_op jit(solution)/shard_map/ppermute | solution.py:12
  211.5 281.7 %reduce-scatter.11.cloned.1.call-start = ((), (), s32[]{:S(2)}) async-start(), calls=%async_computation.12 | async-start | bytes 1064960 | tf_op jit(solution)/shard_map/reduce_scatter | solution.py:174
  214.8 423.0 %reduce-scatter.9.cloned.1.call-start = ((), (), s32[]{:S(2)}) async-start(), calls=%async_computation.11 | async-start | bytes 2129920 | tf_op jit(solution)/shard_map/reduce_scatter | solution.py:174
  219.0 564.5 %reduce-scatter.5.cloned.1.call-start = ((), (), s32[]{:S(2)}) async-start(), calls=%async_computation.9 | async-start | bytes 3194880 | tf_op jit(solution)/shard_map/reduce_scatter | solution.py:174
  229.6 21.5 %copy-start.74 = (f32[512]{0:T(512)S(1)}, f32[512]{0:T(512)}, u32[]{:S(2)}) copy-start(f32[512]{0:T(512)} %get-tuple-element.116) | copy-start | bytes 6148
  229.6 21.4 %copy-start.75 = (f32[512]{0:T(512)S(1)}, f32[512]{0:T(512)}, u32[]{:S(2)}) copy-start(f32[512]{0:T(512)} %get-tuple-element.118) | copy-start | bytes 6148
  229.6 21.4 %copy-start.76 = (f32[512]{0:T(512)S(1)}, f32[512]{0:T(512)}, u32[]{:S(2)}) copy-start(f32[512]{0:T(512)} %get-tuple-element.120) | copy-start | bytes 6148
  229.7 21.4 %copy-start.77 = (f32[512]{0:T(512)S(1)}, f32[512]{0:T(512)}, u32[]{:S(2)}) copy-start(f32[512]{0:T(512)} %get-tuple-element.122) | copy-start | bytes 6148
  229.7 147.2 %copy-start.19 = (bf16[256,512]{1,0:T(8,128)(2,1)S(1)}, bf16[256,512]{1,0:T(8,128)(2,1)}, u32[]{:S(2)}) copy-start(bf16[256,512]{1,0:T(8,128)(2,1)} %fusion.60) | copy-start | bytes 786436
  239.8 144.0 %copy-start.39 = (bf16[64,512]{1,0:T(8,128)(2,1)S(1)}, bf16[64,512]{1,0:T(8,128)(2,1)}, u32[]{:S(2)}) copy-start(bf16[64,512]{1,0:T(8,128)(2,1)} %copy-done.38) | copy-start | bytes 196612
  239.8 144.0 %copy-start.41 = (bf16[64,512]{1,0:T(8,128)(2,1)S(1)}, bf16[64,512]{1,0:T(8,128)(2,1)}, u32[]{:S(2)}) copy-start(bf16[64,512]{1,0:T(8,128)(2,1)} %copy-done.40) | copy-start | bytes 196612
  241.5 139.9 %all-to-all-start.4 = ((bf16[64,2,512]{2,1,0:T(2,128)(2,1)}), bf16[64,2,512]{2,1,0:T(2,128)(2,1)}, u32[]{:S(2)}, u32[]{:S(2)}) async-start(bf16[64,2,512]{2,1,0:T(2,128)(2,1)} %all_to_all.47), calls=%async_computation.4 | async-start | bytes 262144 | tf_op jit(solution)/shard_map/all_to_all | solution.py:152
  (94 other events, 275.0 us)
Sparse Core Ops, SparseCore 0:
  211.6 138.4 reduce-scatter.6
  354.6 138.5 reduce-scatter.10
  497.8 139.8 reduce-scatter.8
  642.3 141.1 reduce-scatter.4
where the time goes:
time: 802 us; the launch traced here: 790 us
  waiting for transfers between devices  434 us (54%)
  blocking collectives  124 us (15%)
  other arithmetic  86.6 us (11%)
  local copies, waits for them, and re-layouts  50.3 us (6%)
  starting transfers between devices  46.9 us (6%)
  matrix products  31.4 us (4%)
  between operations  16.6 us (2%)
    reduce_scatter x4, waiting for transfers between devices, on_device(): lax.psum_scatter(weight_sums, 'dom', scatter_dimension=0, tiled=True)  395 us
    unnamed x1, blocking collectives  124 us
    all_to_all x4, starting transfers between devices, on_device(): lax.all_to_all(source_sums[count_nodes:].astype(jnp.bfloat16), 'dom', spl...  30.7 us
    ppermute x3, waiting for transfers between devices, passed_along(): lax.ppermute(value, axis, [(source, source + steps) for source in range(f...  25.6 us
    unnamed x214, local copies, waits for them, and re-layouts  20.1 us
    dot_general x16, matrix products, contract(): lax.dot_general(former, latter, (((0,), (0,)), ((), ())), preferred_eleme...  16.8 us
    scatter-add x4, other arithmetic, layer_backward(): jax.ops.segment_sum(edge_grad_in[:, 2 * width:], receiver, num_segments=c...  16.1 us
  transfers between devices with their start and end apart: 12, of which 10 were waited for; matrix products, arithmetic and copies ran while one was open for 9% of the time, Pallas kernels for 0%

commit v1 on v0

v1 whole, which is shorter than its diff:
```python
import functools

import jax
import jax.numpy as jnp
from jax import lax
from jax.experimental import pallas as pl
from jax.experimental.pallas import tpu as pltpu
from jax.sharding import PartitionSpec as P

EPS = 1e-05
MESH = pl.DeviceIdType.MESH
F32 = jnp.float32
BF16 = jnp.bfloat16
DOM_Z = 8
DOM_CORE = 2


def passed_along(value, axis, steps):
    count = lax.axis_size(axis)
    first, last = (max(0, -steps), min(count, count - steps))
    return lax.ppermute(value, axis, [(source, source + steps) for source in range(first, last)])


def dot(a, b):
    return jnp.dot(a, b, preferred_element_type=F32)


def dot_t(a, b):
    return lax.dot_general(a, b, (((1,), (1,)), ((), ())), preferred_element_type=F32)


def contract(a, b):
    return lax.dot_general(a, b, (((0,), (0,)), ((), ())), preferred_element_type=F32)


def mean(x):
    return jnp.mean(x, axis=-1, keepdims=True)


def mlp_forward(pre, outer):
    sig = jax.nn.sigmoid(pre)
    act = (pre * sig).astype(BF16)
    out = dot(act, outer)
    centred = out - mean(out)
    rescale = lax.rsqrt(mean(centred * centred) + EPS)
    slope = sig * (1.0 + pre * (1.0 - sig))
    return act, slope, centred * rescale, rescale


def mlp_backward(outer, gain, slope, normed, rescale, cotangent):
    grad_norm = cotangent * gain
    grad_out = rescale * (grad_norm - mean(grad_norm) - normed * mean(grad_norm * normed))
    grad_out = grad_out.astype(BF16)
    grad_pre = (dot_t(grad_out, outer) * slope).astype(BF16)
    return grad_out, grad_pre, jnp.sum(cotangent * normed, axis=0, keepdims=True)


def reduce_kernel(
    dims,
    x_e, pre_e, act_e, out_e, x_n, pre_n, act_n, out_n, gains,
    w1e, w2e, ge, w1n, w2n, gn,
    terms, from_core, chip_sum, from_y, y_sum, from_z,
    sem_core_s, sem_core_r, sem_y_s, sem_y_r, sem_z_s, sem_z_r,
):
    ny, nz = dims
    dom = lax.axis_index("dom")
    core = lax.rem(dom, 2)
    z = lax.rem(lax.div(dom, 2), nz)
    y = lax.div(dom, 2 * nz)

    def at(yy, zz, cc):
        return {"dom": (yy * nz + zz) * 2 + cc}

    barrier = pltpu.get_barrier_semaphore()
    pl.semaphore_signal(barrier, inc=1, device_id=at(y, z, 1 - core), device_id_type=MESH)
    for k in range(1, ny):
        pl.semaphore_signal(
            barrier, inc=1, device_id=at(lax.rem(y + k, ny), z, core), device_id_type=MESH
        )
    for k in range(1, nz):
        pl.semaphore_signal(
            barrier, inc=1, device_id=at(y, lax.rem(z + k, nz), core), device_id_type=MESH
        )

    count = ny * nz * 2
    a1 = w1e.shape[0]
    b1 = w1n.shape[0]
    e1 = contract(x_e[...], pre_e[...])
    e2 = contract(act_e[...], out_e[...])
    n1 = contract(x_n[...], pre_n[...])
    n2 = contract(act_n[...], out_n[...])
    a2 = e2.shape[0] // count
    b2 = n2.shape[0] // count
    gain_rows = gains[...]
    ra = a1 + a2
    rb = ra + b1
    for d in range(count):
        c, yz = d % 2, d // 2
        yy, zz = yz // nz, yz % nz
        terms[c, zz, yy, 0:ra] = jnp.concatenate(
            [e1[a1 * d : a1 * d + a1], e2[a2 * d : a2 * d + a2]], axis=0
        ).astype(BF16)
        terms[c, zz, yy, ra:rb] = n1[b1 * d : b1 * d + b1].astype(BF16)
        terms[c, zz, yy, rb : rb + b2 + 8] = jnp.concatenate(
            [n2[b2 * d : b2 * d + b2], gain_rows], axis=0
        ).astype(BF16)

    pl.semaphore_wait(barrier, ny + nz - 1)

    order = sorted(range(nz), key=lambda k: -min(k, nz - k))
    places = [lax.rem(z + k, nz) for k in order]
    core_copies, y_copies, z_copies = [], [], []
    for i, place in enumerate(places):
        copy = pltpu.make_async_remote_copy(
            src_ref=terms.at[1 - core, place],
            dst_ref=from_core.at[place],
            send_sem=sem_core_s.at[i],
            recv_sem=sem_core_r.at[place],
            device_id=at(y, z, 1 - core),
            device_id_type=MESH,
        )
        copy.start()
    for i, place in enumerate(places):
        pltpu.make_async_remote_copy(
            src_ref=terms.at[1 - core, place],
            dst_ref=from_core.at[place],
            send_sem=sem_core_s.at[i],
            recv_sem=sem_core_r.at[place],
            device_id=at(y, z, 1 - core),
            device_id_type=MESH,
        ).wait_recv()
        chip_sum[i] = (terms[core, place].astype(F32) + from_core[place].astype(F32)).astype(BF16)
        for k in range(1, ny):
            target = lax.rem(y + k, ny)
            copy = pltpu.make_async_remote_copy(
                src_ref=chip_sum.at[i, target],
                dst_ref=from_y.at[i, k - 1],
                send_sem=sem_y_s.at[i, k - 1],
                recv_sem=sem_y_r.at[i, k - 1],
                device_id=at(target, z, core),
                device_id_type=MESH,
            )
            copy.start()
            y_copies.append(copy)
    last = None
    for i, k in enumerate(order):
        for j in range(ny - 1):
            y_copies[i * (ny - 1) + j].wait_recv()
        total = chip_sum[i, y].astype(F32)
        for j in range(ny - 1):
            total = total + from_y[i, j].astype(F32)
        if k == 0:
            last = total
        else:
            y_sum[i] = total.astype(BF16)
            copy = pltpu.make_async_remote_copy(
                src_ref=y_sum.at[i],
                dst_ref=from_z.at[k - 1],
                send_sem=sem_z_s.at[k - 1],
                recv_sem=sem_z_r.at[k - 1],
                device_id=at(y, places[i], core),
                device_id_type=MESH,
            )
            copy.start()
            z_copies.append(copy)
    for copy in z_copies:
        copy.wait_recv()
    for k in range(nz - 1):
        last = last + from_z[k].astype(F32)
    w1e[...] = last[0:a1]
    w2e[...] = last[a1:ra]
    w1n[...] = last[ra:rb]
    w2n[...] = last[rb : rb + b2]
    tail = last[rb + b2 : rb + b2 + 8]
    width = tail.shape[1]
    per = ge.shape[1]
    shifted = pltpu.roll(tail, lax.rem(width - per * dom, width), 1)
    ge[...] = shifted[0:1, 0:per]
    gn[...] = shifted[1:2, 0:per]
    for i, place in enumerate(places):
        pltpu.make_async_remote_copy(
            src_ref=terms.at[1 - core, place],
            dst_ref=from_core.at[place],
            send_sem=sem_core_s.at[i],
            recv_sem=sem_core_r.at[place],
            device_id=at(y, z, 1 - core),
            device_id_type=MESH,
        ).wait_send()
    for copy in y_copies + z_copies:
        copy.wait_send()


def reduced_terms(edge_terms, node_terms, gains):
    count = lax.axis_size("dom")
    nz = min(DOM_Z, count // 4)
    ny = count // (2 * nz)
    x_e, pre_e, act_e, out_e = edge_terms
    x_n, pre_n, act_n, out_n = node_terms
    hid, width = pre_e.shape[1], out_e.shape[1]
    rows = (x_e.shape[1] + 2 * hid + x_n.shape[1]) // count + 8
    vmem = pl.BlockSpec(memory_space=pltpu.VMEM)
    dma = pltpu.SemaphoreType.DMA
    return pl.pallas_call(
        functools.partial(reduce_kernel, (ny, nz)),
        out_shape=(
            jax.ShapeDtypeStruct((x_e.shape[1] // count, hid), F32),
            jax.ShapeDtypeStruct((hid // count, width), F32),
            jax.ShapeDtypeStruct((1, width // count), F32),
            jax.ShapeDtypeStruct((x_n.shape[1] // count, hid), F32),
            jax.ShapeDtypeStruct((hid // count, width), F32),
            jax.ShapeDtypeStruct((1, width // count), F32),
        ),
        in_specs=[vmem] * 9,
        out_specs=[vmem] * 6,
        scratch_shapes=[
            pltpu.VMEM((2, nz, ny, rows, width), BF16),
            pltpu.VMEM((nz, ny, rows, width), BF16),
            pltpu.VMEM((nz, ny, rows, width), BF16),
            pltpu.VMEM((nz, ny - 1, rows, width), BF16),
            pltpu.VMEM((nz, rows, width), BF16),
            pltpu.VMEM((nz - 1, rows, width), BF16),
            dma((nz,)),
            dma((nz,)),
            dma((nz, ny - 1)),
            dma((nz, ny - 1)),
            dma((nz - 1,)),
            dma((nz - 1,)),
        ],
        compiler_params=pltpu.CompilerParams(
            collective_id=0, has_side_effects=True, vmem_limit_bytes=60 * 1024 * 1024
        ),
        name="weight_reduce",
    )(x_e, pre_e, act_e, out_e, x_n, pre_n, act_n, out_n, gains)


def on_device(
    node_states, edge_states, node_cot, edge_cot,
    edge_w1, edge_w2, edge_gain, node_w1, node_w2, node_gain,
    edge_src, edge_dst, edge_count, send_rows,
):
    phases = lax.axis_size("pipe")
    section = lax.axis_index("pipe")
    nodes, width = node_states.shape[2], node_states.shape[3]
    edges = edge_states.shape[2]
    ew1, ew2, nw1, nw2 = edge_w1[0], edge_w2[0], node_w1[0], node_w2[0]
    egain, ngain = edge_gain[0].astype(F32), node_gain[0].astype(F32)
    live = (jnp.arange(edges, dtype=jnp.int32) < edge_count[0]).astype(F32)[:, None]
    outgoing = send_rows[0].reshape(-1)
    ghosts_n = outgoing.shape[0]
    is_top = section == phases - 1
    h = node_states[0, 0]
    e = edge_states[0, 0]
    pick_send = (outgoing[:, None] == jnp.arange(nodes)[None, :]).astype(BF16)
    pick_src = (edge_src[:, None] == jnp.arange(nodes + ghosts_n)[None, :]).astype(BF16)
    pick_dst = (edge_dst[:, None] == jnp.arange(nodes)[None, :]).astype(BF16)
    sent = dot(pick_send, h).astype(BF16)
    ghosts = lax.all_to_all(sent, "dom", split_axis=0, concat_axis=0, tiled=True)
    table = jnp.concatenate([h, ghosts], axis=0)
    x_e = jnp.concatenate(
        [e, dot(pick_src, table).astype(BF16), dot(pick_dst, h).astype(BF16)], axis=1
    )
    act_e, slope_e, normed_e, rescale_e = mlp_forward(dot(x_e, ew1), ew2)
    new_edges = (e.astype(F32) + normed_e * egain) * live
    agg = contract(pick_dst, new_edges.astype(BF16)).astype(BF16)
    x_n = jnp.concatenate([h, agg], axis=1)
    act_n, slope_n, normed_n, rescale_n = mlp_forward(dot(x_n, nw1), nw2)

    carried = jnp.zeros((nodes + edges, width), BF16)
    kept = None
    for tick in range(phases):
        valid = tick == phases - 1 - section
        if tick > 0:
            carried = passed_along(carried, "pipe", -1)
        cn = jnp.where(is_top, node_cot[0], carried[:nodes]).astype(F32)
        ce = jnp.where(is_top, edge_cot[0], carried[nodes:]).astype(F32)
        out_n, pre_n, gain_n = mlp_backward(nw2, ngain, slope_n, normed_n, rescale_n, cn)
        back_n = dot_t(pre_n, nw1)
        g_edges = (ce + dot(pick_dst, back_n[:, width:].astype(BF16))) * live
        out_e, pre_e, gain_e = mlp_backward(ew2, egain, slope_e, normed_e, rescale_e, g_edges)
        by_src = dot_t(contract(pick_src, pre_e).astype(BF16), ew1[width : 2 * width])
        by_dst = dot_t(contract(pick_dst, pre_e).astype(BF16), ew1[2 * width :])
        edge_out = (g_edges + dot_t(pre_e, ew1[:width])).astype(BF16)
        back = lax.all_to_all(
            by_src[nodes:].astype(BF16), "dom", split_axis=0, concat_axis=0, tiled=True
        )
        node_out = (
            cn + back_n[:, :width] + by_dst + by_src[:nodes] + contract(pick_send, back)
        ).astype(BF16)
        carried = jnp.concatenate([node_out, edge_out], axis=0)
        gains = jnp.concatenate([gain_e, gain_n, jnp.zeros((6, width), F32)], axis=0)
        now = (node_out, edge_out, out_n, pre_n, out_e, pre_e, gains)
        if kept is None:
            kept = now
        else:
            kept = tuple(jnp.where(valid, a, b) for a, b in zip(now, kept))
    node_out, edge_out, out_n, pre_n, out_e, pre_e, gains = kept
    w1e, w2e, ge, w1n, w2n, gn = reduced_terms(
        (x_e, pre_e, act_e, out_e), (x_n, pre_n, act_n, out_n), gains
    )
    return (
        node_out[None, None], edge_out[None, None],
        w1e[None], w2e[None], ge, w1n[None], w2n[None], gn,
    )


def solution(mesh):
    placed = (
        P("pipe", None, "dom", None),
        P("pipe", None, "dom", None),
        P(None, "dom", None),
        P(None, "dom", None),
        P("pipe", None, None),
        P("pipe", None, None),
        P("pipe", None),
        P("pipe", None, None),
        P("pipe", None, None),
        P("pipe", None),
        P("dom"),
        P("dom"),
        P("dom"),
        P("dom", None, None),
    )
    return jax.shard_map(
        on_device,
        mesh=mesh,
        in_specs=placed,
        out_specs=(
            P("pipe", None, "dom", None),
            P("pipe", None, "dom", None),
            P("pipe", "dom", None),
            P("pipe", "dom", None),
            P("pipe", "dom"),
            P("pipe", "dom", None),
            P("pipe", "dom", None),
            P("pipe", "dom"),
        ),
        check_vma=False,
    )
```

time: 802 us -> 242 us (0.30); the launches traced: 790 us -> 238 us
  waiting for transfers between devices: 434 us -> 59.1 us
  blocking collectives: 124 us -> 0 us
  other arithmetic: 86.6 us -> 16.2 us
  Pallas kernels: 0 us -> 36.1 us
  matrix products: 31.4 us -> 50.8 us
  local copies, waits for them, and re-layouts: 50.3 us -> 35.9 us
  between operations: 16.6 us -> 2.55 us
  starting transfers between devices: 46.9 us -> 37.6 us
    reduce_scatter x4 -> x0, waiting for transfers between devices: 395 us -> none  [on_device(): lax.psum_scatter(weight_sums, 'dom', scatter_dimension=0, tiled=True)]
    unnamed x1 -> x0, blocking collectives: 124 us -> none
    scatter-add x13 -> x0, other arithmetic: 40.6 us -> none  [the longest x4 16.1 us: layer_backward(): jax.ops.segment_sum(edge_grad_in[:, 2 * width:], receiver, num_segments=c...]
    pallas_call x0 -> x1, Pallas kernels: none -> 36.1 us  [reduced_terms(): pl.pallas_call(functools.partial(reduce_kernel, (ny, nz)), out_shape=(jax...]
    dot_general x36 -> x40, matrix products: 31.4 us -> 50.8 us  [the longest x24 33.8 us: dot_t(): lax.dot_general(a, b, (((1,), (1,)), ((), ())), preferred_element_type=F32)]
    all_to_all x5, waiting for transfers between devices: 13.4 us -> 31.2 us  [the longest x4 24.4 us: on_device(): lax.all_to_all(by_src[nodes:].astype(BF16), 'dom', split_axis=0, concat_a...]
    gather x7 -> x0, local copies, waits for them, and re-layouts: 10.9 us -> none  [the longest x4 6.92 us: layer_backward(): node_grad_in[:, width:][receiver]]
    convert_element_type x12 -> x4, other arithmetic: 10.3 us -> 0.64 us  [the longest x3 0.63 us: mlp_backward(): grad_out = grad_out.astype(BF16)]
  transfers between devices with their start and end apart: 12 -> 8, of which waited for: 10 -> 7; matrix products, arithmetic and copies ran while one was open for 9% -> 7% of each run, Pallas kernels for 0% -> 15%
where the time goes in v1:
time: 242 us; the launch traced here: 238 us
  waiting for transfers between devices  59.1 us (24%)
  matrix products  50.8 us (21%)
  starting transfers between devices  37.6 us (16%)
  Pallas kernels  36.1 us (15%)
  local copies, waits for them, and re-layouts  35.9 us (15%)
  other arithmetic  16.2 us (7%)
  between operations  2.55 us (1%)
    pallas_call x1, Pallas kernels, reduced_terms(): pl.pallas_call(functools.partial(reduce_kernel, (ny, nz)), out_shape=(jax...  36.1 us
    dot_general x24, matrix products, dot_t(): lax.dot_general(a, b, (((1,), (1,)), ((), ())), preferred_element_type=F32)  33.8 us
    ppermute x3, waiting for transfers between devices, passed_along(): lax.ppermute(value, axis, [(source, source + steps) for source in range(f...  27.9 us
    all_to_all x4, waiting for transfers between devices, on_device(): lax.all_to_all(by_src[nodes:].astype(BF16), 'dom', split_axis=0, concat_a...  24.4 us
    all_to_all x4, starting transfers between devices, on_device(): lax.all_to_all(by_src[nodes:].astype(BF16), 'dom', split_axis=0, concat_a...  21.7 us
    unnamed x213, local copies, waits for them, and re-layouts  18.1 us
    all_to_all x1, starting transfers between devices, on_device(): lax.all_to_all(sent, 'dom', split_axis=0, concat_axis=0, tiled=True)  11.8 us
    all_to_all x8, local copies, waits for them, and re-layouts, on_device(): lax.all_to_all(by_src[nodes:].astype(BF16), 'dom', split_axis=0, concat_a...  10.4 us
  transfers between devices with their start and end apart: 8, of which 7 were waited for; matrix products, arithmetic and copies ran while one was open for 7% of the time, Pallas kernels for 15%

profile of v1, /device:TPU:32, one launch (start us, length us, event | category | flops | bytes accessed | tf_op | source)
XLA Modules:
  0.0 238.3 jit_solution(13484378580847354590)
XLA Ops:
  3.5 11.8 %all-to-all-start = ((bf16[64,2,512]{2,1,0:T(2,128)(2,1)}), bf16[64,2,512]{2,1,0:T(2,128)(2,1)S(1)}, u32[]{:S(2)}, u32[]{:S(2)}) async-start(bf16[64,2,512]{2,1,0:T(2,128)(2,1)} %all_to_all.40), calls=%async_computation | async-start | bytes 262144 | tf_op jit(solution)/shard_map/all_to_all | solution.py:257
  18.5 6.8 %all-to-all-done = bf16[64,2,512]{2,1,0:T(2,128)(2,1)S(1)} async-done(((bf16[64,2,512]{2,1,0:T(2,128)(2,1)}), bf16[64,2,512]{2,1,0:T(2,128)(2,1)S(1)}, u32[]{:S(2)}, u32[]{:S(2)}) %all-to-all-start) | async-done | bytes 131104 | tf_op jit(solution)/shard_map/all_to_all | solution.py:257
  35.3 2.0 fusion.13
  40.5 5.5 %all-to-all-start.1 = ((bf16[64,2,512]{2,1,0:T(2,128)(2,1)}), bf16[64,2,512]{2,1,0:T(2,128)(2,1)}, u32[]{:S(2)}, u32[]{:S(2)}) async-start(bf16[64,2,512]{2,1,0:T(2,128)(2,1)} %all_to_all.43), calls=%async_computation.1 | async-start | bytes 262144 | tf_op jit(solution)/shard_map/all_to_all | solution.py:283
  47.5 8.6 %all-to-all-done.1 = bf16[64,2,512]{2,1,0:T(2,128)(2,1)} async-done(((bf16[64,2,512]{2,1,0:T(2,128)(2,1)}), bf16[64,2,512]{2,1,0:T(2,128)(2,1)}, u32[]{:S(2)}, u32[]{:S(2)}) %all-to-all-start.1) | async-done | bytes 131104 | tf_op jit(solution)/shard_map/all_to_all | solution.py:283
  59.6 2.2 fusion.20
  64.1 10.3 %collective-permute-done = bf16[320,512]{1,0:T(8,128)(2,1)S(1)} collective-permute-done((bf16[320,512]{1,0:T(8,128)(2,1)S(1)}, bf16[320,512]{1,0:T(8,128)(2,1)S(1)}, u32[]{:S(2)}, u32[]{:S(2)}) %collective-permute-start) | collective-permute-done | bytes 327712 | tf_op jit(solution)/shard_map/ppermute | solution.py:21
  82.9 2.2 fusion.14
  85.2 2.1 fusion.27
  90.5 5.5 %all-to-all-start.2 = ((bf16[64,2,512]{2,1,0:T(2,128)(2,1)}), bf16[64,2,512]{2,1,0:T(2,128)(2,1)}, u32[]{:S(2)}, u32[]{:S(2)}) async-start(bf16[64,2,512]{2,1,0:T(2,128)(2,1)} %all_to_all.46), calls=%async_computation.2 | async-start | bytes 262144 | tf_op jit(solution)/shard_map/all_to_all | solution.py:283
  96.0 2.1 fusion.6
  98.2 7.9 %all-to-all-done.2 = bf16[64,2,512]{2,1,0:T(2,128)(2,1)} async-done(((bf16[64,2,512]{2,1,0:T(2,128)(2,1)}), bf16[64,2,512]{2,1,0:T(2,128)(2,1)}, u32[]{:S(2)}, u32[]{:S(2)}) %all-to-all-start.2) | async-done | bytes 131104 | tf_op jit(solution)/shard_map/all_to_all | solution.py:283
  113.6 9.8 %collective-permute-done.1 = bf16[320,512]{1,0:T(8,128)(2,1)} collective-permute-done((bf16[320,512]{1,0:T(8,128)(2,1)}, bf16[320,512]{1,0:T(8,128)(2,1)}, u32[]{:S(2)}, u32[]{:S(2)}) %collective-permute-start.1) | collective-permute-done | bytes 327712 | tf_op jit(solution)/shard_map/ppermute | solution.py:21
  128.1 2.2 multiply_reduce_fusion.2
  133.0 2.2 fusion.15
  135.3 2.1 fusion.28
  140.6 5.5 %all-to-all-start.3 = ((bf16[64,2,512]{2,1,0:T(2,128)(2,1)}), bf16[64,2,512]{2,1,0:T(2,128)(2,1)}, u32[]{:S(2)}, u32[]{:S(2)}) async-start(bf16[64,2,512]{2,1,0:T(2,128)(2,1)} %all_to_all.49), calls=%async_computation.3 | async-start | bytes 262144 | tf_op jit(solution)/shard_map/all_to_all | solution.py:283
  146.1 2.2 fusion.8
  148.3 7.9 %all-to-all-done.3 = bf16[64,2,512]{2,1,0:T(2,128)(2,1)} async-done(((bf16[64,2,512]{2,1,0:T(2,128)(2,1)}), bf16[64,2,512]{2,1,0:T(2,128)(2,1)}, u32[]{:S(2)}, u32[]{:S(2)}) %all-to-all-start.3) | async-done | bytes 131104 | tf_op jit(solution)/shard_map/all_to_all | solution.py:283
  164.3 7.8 %collective-permute-done.2 = bf16[320,512]{1,0:T(8,128)(2,1)S(1)} collective-permute-done((bf16[320,512]{1,0:T(8,128)(2,1)S(1)}, bf16[320,512]{1,0:T(8,128)(2,1)S(1)}, u32[]{:S(2)}, u32[]{:S(2)}) %collective-permute-start.2) | collective-permute-done | bytes 327712 | tf_op jit(solution)/shard_map/ppermute | solution.py:21
  179.8 2.3 fusion.16
  183.7 5.1 %all-to-all-start.4 = ((bf16[64,2,512]{2,1,0:T(2,128)(2,1)}), bf16[64,2,512]{2,1,0:T(2,128)(2,1)S(1)}, u32[]{:S(2)}, u32[]{:S(2)}) async-start(bf16[64,2,512]{2,1,0:T(2,128)(2,1)} %all_to_all.52), calls=%async_computation.4 | async-start | bytes 262144 | tf_op jit(solution)/shard_map/all_to_all | solution.py:283
  190.3 2.2 fusion.12
  192.5 36.1 %weight_reduce.1 = (f32[24,512]{1,0:T(8,128)}, f32[8,512]{1,0:T(8,128)}, f32[1,8]{1,0:T(1,128)}, f32[16,512]{1,0:T(8,128)}, f32[8,512]{1,0:T(8,128)}, /*index=5*/f32[1,8]{1,0:T(1,128)}) custom-call(bf16[256,1536]{1,0:T(8,128)(2,1)} %pad_maximum_fusion.x_e, bf16[256,512]{1,0:T(8,128)(2,1)} %get-tuple-element.61.pre_e, bf16[256,512]{1,0:T(8,128)(2,1)} %copy-done.26, ...), custom_call_target="tpu_custom_call" | custom-call | tf_op jit(solution)/shard_map/weight_reduce/pallas_call | solution.py:203
  (302 shorter events, 83.3 us)
Async XLA Ops:
  0.6 28.2 %copy-start = (bf16[1,1024,512]{2,1,0:T(8,128)(2,1)S(1)}, bf16[1,1024,512]{2,1,0:T(8,128)(2,1)}, u32[]{:S(2)}) copy-start(bf16[1,1024,512]{2,1,0:T(8,128)(2,1)} %param.21) | copy-start | bytes 3145732
  0.6 25.9 %copy-start.1 = (bf16[1,1536,512]{2,1,0:T(8,128)(2,1)S(1)}, bf16[1,1536,512]{2,1,0:T(8,128)(2,1)}, u32[]{:S(2)}) copy-start(bf16[1,1536,512]{2,1,0:T(8,128)(2,1)} %param.18) | copy-start | bytes 4718596
  0.7 25.9 %copy-start.17 = (bf16[1,1,256,512]{3,2,1,0:T(8,128)(2,1)S(1)}, bf16[1,1,256,512]{3,2,1,0:T(8,128)(2,1)}, u32[]{:S(2)}) copy-start(bf16[1,1,256,512]{3,2,1,0:T(8,128)(2,1)} %param.15) | copy-start | bytes 786436
  1.7 15.6 %copy-start.66 = (s32[128]{0:T(128)}, s32[128]{0:T(128)S(1)}, u32[]{:S(2)}) copy-start(s32[128]{0:T(128)S(1)} %eq.61) | copy-start | bytes 1540
  3.5 21.8 %all-to-all-start = ((bf16[64,2,512]{2,1,0:T(2,128)(2,1)}), bf16[64,2,512]{2,1,0:T(2,128)(2,1)S(1)}, u32[]{:S(2)}, u32[]{:S(2)}) async-start(bf16[64,2,512]{2,1,0:T(2,128)(2,1)} %all_to_all.40), calls=%async_computation | async-start | bytes 262144 | tf_op jit(solution)/shard_map/all_to_all | solution.py:257
  40.5 15.6 %all-to-all-start.1 = ((bf16[64,2,512]{2,1,0:T(2,128)(2,1)}), bf16[64,2,512]{2,1,0:T(2,128)(2,1)}, u32[]{:S(2)}, u32[]{:S(2)}) async-start(bf16[64,2,512]{2,1,0:T(2,128)(2,1)} %all_to_all.43), calls=%async_computation.1 | async-start | bytes 262144 | tf_op jit(solution)/shard_map/all_to_all | solution.py:283
  62.7 16.4 %copy-start.61 = (s32[256]{0:T(256)S(1)}, s32[256]{0:T(256)}, u32[]{:S(2)}) copy-start(s32[256]{0:T(256)} %param.25) | copy-start | bytes 3076
  62.7 16.4 %copy-start.81 = (f32[256]{0:T(256)S(1)}, f32[256]{0:T(256)}, u32[]{:S(2)}) copy-start(f32[256]{0:T(256)} %copy-done.79) | copy-start | bytes 3076
  62.7 16.4 %copy-start.92 = (bf16[1,256,512]{2,1,0:T(8,128)(2,1)S(1)}, bf16[1,256,512]{2,1,0:T(8,128)(2,1)}, u32[]{:S(2)}) copy-start(bf16[1,256,512]{2,1,0:T(8,128)(2,1)} %param.17) | copy-start | bytes 786436
  62.7 11.8 %collective-permute-start = (bf16[320,512]{1,0:T(8,128)(2,1)S(1)}, bf16[320,512]{1,0:T(8,128)(2,1)S(1)}, u32[]{:S(2)}, u32[]{:S(2)}) collective-permute-start(bf16[320,512]{1,0:T(8,128)(2,1)S(1)} %pad_maximum_fusion.1), channel_id=1, source_target_pairs={{64,0},{128,64},{192,128},{65,1},{129,65},{193,129},{66,2},{130,66... | collective-permute-start | bytes 983048 | tf_op jit(solution)/shard_map/ppermute | solution.py:21
  90.5 15.6 %all-to-all-start.2 = ((bf16[64,2,512]{2,1,0:T(2,128)(2,1)}), bf16[64,2,512]{2,1,0:T(2,128)(2,1)}, u32[]{:S(2)}, u32[]{:S(2)}) async-start(bf16[64,2,512]{2,1,0:T(2,128)(2,1)} %all_to_all.46), calls=%async_computation.2 | async-start | bytes 262144 | tf_op jit(solution)/shard_map/all_to_all | solution.py:283
  111.4 11.9 %collective-permute-start.1 = (bf16[320,512]{1,0:T(8,128)(2,1)}, bf16[320,512]{1,0:T(8,128)(2,1)}, u32[]{:S(2)}, u32[]{:S(2)}) collective-permute-start(bf16[320,512]{1,0:T(8,128)(2,1)} %pad_maximum_fusion.2), channel_id=1, source_target_pairs={{64,0},{128,64},{192,128},{65,1},{129,65},{193,129},{66,2},{130,66... | collective-permute-start | bytes 983048 | tf_op jit(solution)/shard_map/ppermute | solution.py:21
  112.9 15.1 %copy-start.93 = (bf16[1,256,512]{2,1,0:T(8,128)(2,1)S(1)}, bf16[1,256,512]{2,1,0:T(8,128)(2,1)}, u32[]{:S(2)}) copy-start(bf16[1,256,512]{2,1,0:T(8,128)(2,1)} %param.17) | copy-start | bytes 786436
  140.6 15.6 %all-to-all-start.3 = ((bf16[64,2,512]{2,1,0:T(2,128)(2,1)}), bf16[64,2,512]{2,1,0:T(2,128)(2,1)}, u32[]{:S(2)}, u32[]{:S(2)}) async-start(bf16[64,2,512]{2,1,0:T(2,128)(2,1)} %all_to_all.49), calls=%async_computation.3 | async-start | bytes 262144 | tf_op jit(solution)/shard_map/all_to_all | solution.py:283
  160.4 11.6 %collective-permute-start.2 = (bf16[320,512]{1,0:T(8,128)(2,1)S(1)}, bf16[320,512]{1,0:T(8,128)(2,1)S(1)}, u32[]{:S(2)}, u32[]{:S(2)}) collective-permute-start(bf16[320,512]{1,0:T(8,128)(2,1)S(1)} %pad_maximum_fusion.3), channel_id=1, source_target_pairs={{64,0},{128,64},{192,128},{65,1},{129,65},{193,129},{66,2},{130,66... | collective-permute-start | bytes 983048 | tf_op jit(solution)/shard_map/ppermute | solution.py:21
  183.7 46.1 %all-to-all-start.4 = ((bf16[64,2,512]{2,1,0:T(2,128)(2,1)}), bf16[64,2,512]{2,1,0:T(2,128)(2,1)S(1)}, u32[]{:S(2)}, u32[]{:S(2)}) async-start(bf16[64,2,512]{2,1,0:T(2,128)(2,1)} %all_to_all.52), calls=%async_computation.4 | async-start | bytes 262144 | tf_op jit(solution)/shard_map/all_to_all | solution.py:283
  190.3 38.4 %copy-start.63 = (s32[256]{0:T(256)S(1)}, s32[256]{0:T(256)}, u32[]{:S(2)}) copy-start(s32[256]{0:T(256)} %param.25) | copy-start | bytes 3076
  192.4 36.2 %copy-start.6 = (bf16[256,512]{1,0:T(8,128)(2,1)S(1)}, bf16[256,512]{1,0:T(8,128)(2,1)}, u32[]{:S(2)}) copy-start(bf16[256,512]{1,0:T(8,128)(2,1)} %get-tuple-element.62) | copy-start | bytes 786436
  192.4 37.4 %copy-start.32 = (bf16[64,512]{1,0:T(8,128)(2,1)S(1)}, bf16[64,512]{1,0:T(8,128)(2,1)}, u32[]{:S(2)}) copy-start(bf16[64,512]{1,0:T(8,128)(2,1)} %fusion.20) | copy-start | bytes 196612
  192.4 37.4 %copy-start.34 = (bf16[64,512]{1,0:T(8,128)(2,1)S(1)}, bf16[64,512]{1,0:T(8,128)(2,1)}, u32[]{:S(2)}) copy-start(bf16[64,512]{1,0:T(8,128)(2,1)} %copy-done.33) | copy-start | bytes 196612
  192.4 37.4 %copy-start.36 = (bf16[64,512]{1,0:T(8,128)(2,1)S(1)}, bf16[64,512]{1,0:T(8,128)(2,1)}, u32[]{:S(2)}) copy-start(bf16[64,512]{1,0:T(8,128)(2,1)} %copy-done.35) | copy-start | bytes 196612
  192.5 37.4 %copy-start.38 = (f32[64,1024]{1,0:T(8,128)S(1)}, f32[64,1024]{1,0:T(8,128)}, u32[]{:S(2)}) copy-start(f32[64,1024]{1,0:T(8,128)} %copy-done.37) | copy-start | bytes 786436
  192.5 37.4 %copy-start.42 = (bf16[64,512]{1,0:T(8,128)(2,1)S(1)}, bf16[64,512]{1,0:T(8,128)(2,1)}, u32[]{:S(2)}) copy-start(bf16[64,512]{1,0:T(8,128)(2,1)} %copy-done.41) | copy-start | bytes 196612
  192.5 37.4 %copy-start.67 = (s32[128]{0:T(128)S(1)}, s32[128]{0:T(128)}, u32[]{:S(2)}) copy-start(s32[128]{0:T(128)} %copy-done.66) | copy-start | bytes 1540
  (87 other events, 401.0 us)

commit v2 on v1

v2 whole, which is shorter than its diff:
```python
import functools

import jax
import jax.numpy as jnp
from jax import lax
from jax.experimental import pallas as pl
from jax.experimental.pallas import tpu as pltpu
from jax.sharding import PartitionSpec as P

EPS = 1e-05
MESH = pl.DeviceIdType.MESH
F32 = jnp.float32
BF16 = jnp.bfloat16
DOM_Z = 8
DOM_CORE = 2


def dot(a, b):
    return jnp.dot(a, b, preferred_element_type=F32)


def dot_t(a, b):
    return lax.dot_general(a, b, (((1,), (1,)), ((), ())), preferred_element_type=F32)


def contract(a, b):
    return lax.dot_general(a, b, (((0,), (0,)), ((), ())), preferred_element_type=F32)


def mean(x):
    return jnp.mean(x, axis=-1, keepdims=True)


def one_hot(rows, index):
    places = lax.broadcasted_iota(jnp.int32, (rows, index.shape[1]), 0)
    return jnp.where(places == index, 1.0, 0.0).astype(BF16)


def mlp_forward(pre, outer):
    sig = jax.nn.sigmoid(pre)
    act = (pre * sig).astype(BF16)
    out = dot(act, outer)
    centred = out - mean(out)
    rescale = lax.rsqrt(mean(centred * centred) + EPS)
    slope = sig * (1.0 + pre * (1.0 - sig))
    return act, slope, centred * rescale, rescale


def mlp_backward(outer, gain, slope, normed, rescale, cotangent):
    grad_norm = cotangent * gain
    grad_out = rescale * (grad_norm - mean(grad_norm) - normed * mean(grad_norm * normed))
    grad_out = grad_out.astype(BF16)
    grad_pre = (dot_t(grad_out, outer) * slope).astype(BF16)
    return grad_out, grad_pre


def layer_kernel(
    dims,
    h_ref, e_ref, ncot_ref, ecot_ref, ew1, ew2, egain, nw1, nw2, ngain, src_ref, dst_ref, count_ref, out_ref,
    node_out, edge_out, w1e, w2e, ge, w1n, w2n, gn,
    rows_f32, send_a, recv_a, send_b, recv_b, node_in, edge_in,
    terms, from_core, chip_sum, from_y, y_sum, from_z,
    sem_a, sem_b, sem_down, sem_up,
    sem_core_s, sem_core_r, sem_y_s, sem_y_r, sem_z_s, sem_z_r,
):
    phases, ny, nz = dims
    count = ny * nz * 2
    dom = lax.axis_index("dom")
    pipe = lax.axis_index("pipe")
    core = lax.rem(dom, 2)
    z = lax.rem(lax.div(dom, 2), nz)
    y = lax.div(dom, 2 * nz)
    nodes, width = h_ref.shape
    edges = e_ref.shape[0]

    def at(yy, zz, cc):
        return {"dom": (yy * nz + zz) * 2 + cc}

    barrier = pltpu.get_barrier_semaphore()

    def greet(k, carry):
        pl.semaphore_signal(
            barrier, inc=1, device_id={"dom": lax.rem(dom + k, count)}, device_id_type=MESH
        )
        return carry

    lax.fori_loop(1, count, greet, 0)
    pl.semaphore_signal(
        barrier, inc=1, device_id={"pipe": lax.rem(pipe + 1, phases)}, device_id_type=MESH
    )
    pl.semaphore_signal(
        barrier, inc=1, device_id={"pipe": lax.rem(pipe + phases - 1, phases)}, device_id_type=MESH
    )

    def spread(value, send):
        rows_f32[...] = value
        for q in range(count):
            send[q] = rows_f32[2 * q : 2 * q + 2].astype(BF16)

    def exchange(send, recv, sem):
        own = pltpu.make_async_copy(send.at[dom], recv.at[dom], sem.at[1])
        own.start()

        def go(k, carry):
            target = lax.rem(dom + k, count)
            pltpu.make_async_remote_copy(
                src_ref=send.at[target],
                dst_ref=recv.at[dom],
                send_sem=sem.at[0],
                recv_sem=sem.at[1],
                device_id={"dom": target},
                device_id_type=MESH,
            ).start()
            return carry

        lax.fori_loop(1, count, go, 0)

    def arrived(recv, sem):
        pltpu.make_async_copy(recv, recv, sem.at[1]).wait()
        for q in range(count):
            rows_f32[2 * q : 2 * q + 2] = recv[q].astype(F32)
        return rows_f32[...].astype(BF16)

    def departed(send, sem):
        part = send.at[pl.ds(0, count - 1)]
        pltpu.make_async_copy(part, part, sem.at[0]).wait()

    h = h_ref[...]
    e = e_ref[...]
    to_send = one_hot(nodes, out_ref[...])
    by_dst = one_hot(nodes, dst_ref[...])
    by_src = one_hot(nodes + 2 * count, src_ref[...])
    spread(contract(to_send, h), send_a)
    pl.semaphore_wait(barrier, count + 1)
    exchange(send_a, recv_a, sem_a)

    live = jnp.where(
        lax.broadcasted_iota(jnp.int32, (edges, width), 0) < count_ref[...], 1.0, 0.0
    )
    gain_e = egain[...].astype(F32)
    gain_n = ngain[...].astype(F32)
    x_dst = contract(by_dst, h).astype(BF16)
    pick_dst = jnp.transpose(by_dst.astype(F32)).astype(BF16)
    pre_e = dot(e, ew1[0:width]) + dot(x_dst, ew1[2 * width : 3 * width])
    ghosts = arrived(recv_a, sem_a)
    x_src = contract(by_src, jnp.concatenate([h, ghosts], axis=0)).astype(BF16)
    pre_e = pre_e + dot(x_src, ew1[width : 2 * width])
    act_e, slope_e, normed_e, rescale_e = mlp_forward(pre_e, ew2[...])
    new_edges = (e.astype(F32) + normed_e * gain_e) * live
    agg = dot(by_dst, new_edges.astype(BF16)).astype(BF16)
    pre_n = dot(h, nw1[0:width]) + dot(agg, nw1[width : 2 * width])
    act_n, slope_n, normed_n, rescale_n = mlp_forward(pre_n, nw2[...])

    below = {"pipe": lax.rem(pipe + phases - 1, phases)}
    node_down = pltpu.make_async_remote_copy(
        src_ref=node_out, dst_ref=node_in, send_sem=sem_down.at[0], recv_sem=sem_down.at[1],
        device_id=below, device_id_type=MESH,
    )
    edge_down = pltpu.make_async_remote_copy(
        src_ref=edge_out, dst_ref=edge_in, send_sem=sem_up.at[0], recv_sem=sem_up.at[1],
        device_id=below, device_id_type=MESH,
    )

    @pl.when(pipe == phases - 1)
    def _():
        node_in[...] = ncot_ref[...]
        edge_in[...] = ecot_ref[...]

    @pl.when(pipe < phases - 1)
    def _():
        node_down.wait_recv()

    cot_n = node_in[...].astype(F32)
    g_out_n, g_pre_n = mlp_backward(nw2[...], gain_n, slope_n, normed_n, rescale_n, cot_n)
    back_agg = dot_t(g_pre_n, nw1[width : 2 * width]).astype(BF16)
    picked = dot(pick_dst, back_agg)

    @pl.when(pipe < phases - 1)
    def _():
        edge_down.wait_recv()

    g_edges = (edge_in[...].astype(F32) + picked) * live
    g_out_e, g_pre_e = mlp_backward(ew2[...], gain_e, slope_e, normed_e, rescale_e, g_edges)
    pre_src = dot(by_src, g_pre_e).astype(BF16)
    spread(dot_t(pre_src[nodes:], ew1[width : 2 * width]), send_b)
    exchange(send_b, recv_b, sem_b)
    edge_out[...] = (g_edges + dot_t(g_pre_e, ew1[0:width])).astype(BF16)

    @pl.when(pipe > 0)
    def _():
        edge_down.start()

    pre_dst = dot(by_dst, g_pre_e).astype(BF16)
    node_part = (
        cot_n
        + dot_t(g_pre_n, nw1[0:width])
        + dot_t(pre_src[:nodes], ew1[width : 2 * width])
        + dot_t(pre_dst, ew1[2 * width : 3 * width])
    )

    a1, b1 = w1e.shape[0], w1n.shape[0]
    a2, b2 = w2e.shape[0], w2n.shape[0]
    gain_rows = jnp.concatenate(
        [
            jnp.sum(g_edges * normed_e, axis=0, keepdims=True),
            jnp.sum(cot_n * normed_n, axis=0, keepdims=True),
            jnp.zeros((6, width), F32),
        ],
        axis=0,
    )
    e1 = jnp.concatenate(
        [contract(e, g_pre_e), contract(x_src, g_pre_e), contract(x_dst, g_pre_e)], axis=0
    )
    e2 = contract(act_e, g_out_e)
    n1 = jnp.concatenate([contract(h, g_pre_n), contract(agg, g_pre_n)], axis=0)
    n2 = contract(act_n, g_out_n)
    ra = a1 + a2
    rb = ra + b1
    for d in range(count):
        c, yz = d % 2, d // 2
        yy, zz = yz // nz, yz % nz
        terms[c, zz, yy, 0:ra] = jnp.concatenate(
            [e1[a1 * d : a1 * d + a1], e2[a2 * d : a2 * d + a2]], axis=0
        ).astype(BF16)
        terms[c, zz, yy, ra:rb] = n1[b1 * d : b1 * d + b1].astype(BF16)
        terms[c, zz, yy, rb : rb + b2 + 8] = jnp.concatenate(
            [n2[b2 * d : b2 * d + b2], gain_rows], axis=0
        ).astype(BF16)

    order = sorted(range(nz), key=lambda k: -min(k, nz - k))
    places = [lax.rem(z + k, nz) for k in order]
    core_copies, y_copies, z_copies = [], [], []
    for i, place in enumerate(places):
        copy = pltpu.make_async_remote_copy(
            src_ref=terms.at[1 - core, place],
            dst_ref=from_core.at[i],
            send_sem=sem_core_s.at[i],
            recv_sem=sem_core_r.at[i],
            device_id=at(y, z, 1 - core),
            device_id_type=MESH,
        )
        copy.start()
        core_copies.append(copy)

    back = arrived(recv_b, sem_b)
    node_out[...] = (node_part + dot(to_send, back)).astype(BF16)

    @pl.when(pipe > 0)
    def _():
        node_down.start()

    for i, place in enumerate(places):
        core_copies[i].wait_recv()
        chip_sum[i] = (terms[core, place].astype(F32) + from_core[i].astype(F32)).astype(BF16)
        for k in range(1, ny):
            target = lax.rem(y + k, ny)
            copy = pltpu.make_async_remote_copy(
                src_ref=chip_sum.at[i, target],
                dst_ref=from_y.at[i, k - 1],
                send_sem=sem_y_s.at[i, k - 1],
                recv_sem=sem_y_r.at[i, k - 1],
                device_id=at(target, z, core),
                device_id_type=MESH,
            )
            copy.start()
            y_copies.append(copy)
    last = None
    for i, k in enumerate(order):
        for j in range(ny - 1):
            y_copies[i * (ny - 1) + j].wait_recv()
        total = chip_sum[i, y].astype(F32)
        for j in range(ny - 1):
            total = total + from_y[i, j].astype(F32)
        if k == 0:
            last = total
        else:
            y_sum[i] = total.astype(BF16)
            copy = pltpu.make_async_remote_copy(
                src_ref=y_sum.at[i],
                dst_ref=from_z.at[k - 1],
                send_sem=sem_z_s.at[k - 1],
                recv_sem=sem_z_r.at[k - 1],
                device_id=at(y, places[i], core),
                device_id_type=MESH,
            )
            copy.start()
            z_copies.append(copy)
    for copy in z_copies:
        copy.wait_recv()
    for k in range(nz - 1):
        last = last + from_z[k].astype(F32)
    w1e[...] = last[0:a1]
    w2e[...] = last[a1:ra]
    w1n[...] = last[ra:rb]
    w2n[...] = last[rb : rb + b2]
    tail = last[rb + b2 : rb + b2 + 8]
    per = ge.shape[1]
    shifted = pltpu.roll(tail, lax.rem(width - per * dom, width), 1)
    ge[...] = shifted[0:1, 0:per]
    gn[...] = shifted[1:2, 0:per]
    departed(send_a, sem_a)
    departed(send_b, sem_b)

    @pl.when(pipe > 0)
    def _():
        node_down.wait_send()
        edge_down.wait_send()

    for copy in core_copies + y_copies + z_copies:
        copy.wait_send()


def on_device(
    node_states, edge_states, node_cot, edge_cot,
    edge_w1, edge_w2, edge_gain, node_w1, node_w2, node_gain,
    edge_src, edge_dst, edge_count, send_rows,
):
    phases = lax.axis_size("pipe")
    count = lax.axis_size("dom")
    nz = min(DOM_Z, count // 4)
    ny = count // (2 * nz)
    nodes, width = node_states.shape[2:]
    edges = edge_states.shape[2]
    hid = edge_w2.shape[1]
    a1, a2, b1 = edge_w1.shape[1] // count, hid // count, node_w1.shape[1] // count
    rows = a1 + 2 * a2 + b1 + 8
    vmem = pl.BlockSpec(memory_space=pltpu.VMEM)
    dma = pltpu.SemaphoreType.DMA

    def shape(*sizes, kind=F32):
        return jax.ShapeDtypeStruct(sizes, kind)

    node_out, edge_out, w1e, w2e, ge, w1n, w2n, gn = pl.pallas_call(
        functools.partial(layer_kernel, (phases, ny, nz)),
        out_shape=(
            shape(nodes, width, kind=BF16),
            shape(edges, width, kind=BF16),
            shape(a1, hid),
            shape(a2, width),
            shape(1, width // count),
            shape(b1, hid),
            shape(a2, width),
            shape(1, width // count),
        ),
        in_specs=[vmem] * 14,
        out_specs=[vmem] * 8,
        scratch_shapes=[
            pltpu.VMEM((2 * count, width), F32),
            pltpu.VMEM((count, 2, width), BF16),
            pltpu.VMEM((count, 2, width), BF16),
            pltpu.VMEM((count, 2, width), BF16),
            pltpu.VMEM((count, 2, width), BF16),
            pltpu.VMEM((nodes, width), BF16),
            pltpu.VMEM((edges, width), BF16),
            pltpu.VMEM((2, nz, ny, rows, width), BF16),
            pltpu.VMEM((nz, ny, rows, width), BF16),
            pltpu.VMEM((nz, ny, rows, width), BF16),
            pltpu.VMEM((nz, ny - 1, rows, width), BF16),
            pltpu.VMEM((nz, rows, width), BF16),
            pltpu.VMEM((nz - 1, rows, width), BF16),
            dma((2,)),
            dma((2,)),
            dma((2,)),
            dma((2,)),
            dma((nz,)),
            dma((nz,)),
            dma((nz, ny - 1)),
            dma((nz, ny - 1)),
            dma((nz - 1,)),
            dma((nz - 1,)),
        ],
        compiler_params=pltpu.CompilerParams(
            collective_id=0, has_side_effects=True, vmem_limit_bytes=60 * 1024 * 1024
        ),
        name="relay_backward",
    )(
        node_states[0, 0], edge_states[0, 0], node_cot[0], edge_cot[0],
        edge_w1[0], edge_w2[0], edge_gain, node_w1[0], node_w2[0], node_gain,
        edge_src[None], edge_dst[None], edge_count[None], send_rows.reshape(1, 2 * count),
    )
    return (
        node_out[None, None], edge_out[None, None],
        w1e[None], w2e[None], ge, w1n[None], w2n[None], gn,
    )


def solution(mesh):
    placed = (
        P("pipe", None, "dom", None),
        P("pipe", None, "dom", None),
        P(None, "dom", None),
        P(None, "dom", None),
        P("pipe", None, None),
        P("pipe", None, None),
        P("pipe", None),
        P("pipe", None, None),
        P("pipe", None, None),
        P("pipe", None),
        P("dom"),
        P("dom"),
        P("dom"),
        P("dom", None, None),
    )
    return jax.shard_map(
        on_device,
        mesh=mesh,
        in_specs=placed,
        out_specs=(
            P("pipe", None, "dom", None),
            P("pipe", None, "dom", None),
            P("pipe", "dom", None),
            P("pipe", "dom", None),
            P("pipe", "dom"),
            P("pipe", "dom", None),
            P("pipe", "dom", None),
            P("pipe", "dom"),
        ),
        check_vma=False,
    )
```

time: 242 us -> 109 us (0.45); the launches traced: 238 us -> 108 us
  waiting for transfers between devices: 59.1 us -> 0 us
  Pallas kernels: 36.1 us -> 94.5 us
  matrix products: 50.8 us -> 0 us
  starting transfers between devices: 37.6 us -> 0 us
  local copies, waits for them, and re-layouts: 35.9 us -> 12.4 us
  other arithmetic: 16.2 us -> 0 us
    pallas_call x1, Pallas kernels: 36.1 us -> 94.5 us  [on_device(): pl.pallas_call(functools.partial(layer_kernel, (phases, ny, nz)), out_sha...]
    dot_general x40 -> x0, matrix products: 50.8 us -> none  [the longest x24 33.8 us: dot_t(): lax.dot_general(a, b, (((1,), (1,)), ((), ())), preferred_element_type=F32)]
    all_to_all x5 -> x0, starting transfers between devices: 33.4 us -> none  [the longest x4 21.7 us: on_device(): lax.all_to_all(by_src[nodes:].astype(BF16), 'dom', split_axis=0, concat_a...]
    all_to_all x5 -> x0, waiting for transfers between devices: 31.2 us -> none  [the longest x4 24.4 us: on_device(): lax.all_to_all(by_src[nodes:].astype(BF16), 'dom', split_axis=0, concat_a...]
    ppermute x3 -> x0, waiting for transfers between devices: 27.9 us -> none  [passed_along(): lax.ppermute(value, axis, [(source, source + steps) for source in range(f...]
    all_to_all x10 -> x0, local copies, waits for them, and re-layouts: 11.2 us -> none  [the longest x8 10.4 us: on_device(): lax.all_to_all(by_src[nodes:].astype(BF16), 'dom', split_axis=0, concat_a...]
    unnamed x213 -> x9, local copies, waits for them, and re-layouts: 18.1 us -> 11.7 us
    concatenate x5 -> x0, other arithmetic: 6.08 us -> none  [the longest x3 3.61 us: on_device(): carried = jnp.concatenate([node_out, edge_out], axis=0)]
  transfers between devices with their start and end apart: 8 -> 0, of which waited for: 7 -> 0; matrix products, arithmetic and copies ran while one was open for 7% -> 0% of each run, Pallas kernels for 15% -> 0%
where the time goes in v2:
time: 109 us; the launch traced here: 108 us
  Pallas kernels  94.5 us (87%)
  local copies, waits for them, and re-layouts  12.4 us (11%)
  between operations  1.29 us (1%)
    pallas_call x1, Pallas kernels, on_device(): pl.pallas_call(functools.partial(layer_kernel, (phases, ny, nz)), out_sha...  94.5 us
    unnamed x9, local copies, waits for them, and re-layouts  11.7 us

profile of v2, /device:TPU:32, one launch (start us, length us, event | category | flops | bytes accessed | tf_op | source)
XLA Modules:
  0.0 108.2 jit_solution(14045933001756704205)
XLA Ops:
  1.3 0.8 copy.23
  2.0 0.7 reshape.19.out_ref
  2.7 94.5 %relay_backward.1 = (bf16[64,512]{1,0:T(8,128)(2,1)}, bf16[256,512]{1,0:T(8,128)(2,1)}, f32[24,512]{1,0:T(8,128)}, f32[8,512]{1,0:T(8,128)}, f32[1,8]{1,0:T(1,12...) custom-call(bf16[64,512]{1,0:T(8,128)(2,1)} %bitcast.25, bf16[256,512]{1,0:T(8,128)(2,1)} %bitcast.22, ...), custom_call_target="tpu_custom_call" | custom-call | tf_op jit(solution)/shard_map/relay_backward/pallas_call | solution.py:333
  97.3 1.5 %copy.33 = bf16[1,1,64,512]{3,2,1,0:T(8,128)(2,1)} copy(bf16[1,1,64,512]{3,2,1,0:T(8,128)(2,1)} %bitcast.27) | data formatting | bytes 131072
  98.7 1.7 %copy.34 = bf16[1,1,256,512]{3,2,1,0:T(8,128)(2,1)} copy(bf16[1,1,256,512]{3,2,1,0:T(8,128)(2,1)} %bitcast.24) | data formatting | bytes 524288
  100.4 1.4 %copy.35 = f32[1,24,512]{2,1,0:T(8,128)} copy(f32[1,24,512]{2,1,0:T(8,128)} %bitcast.28) | data formatting | bytes 98304
  101.8 1.3 %copy.36 = f32[1,8,512]{2,1,0:T(8,128)} copy(f32[1,8,512]{2,1,0:T(8,128)} %bitcast.31) | data formatting | bytes 32768
  103.1 1.2 %copy.37 = f32[1,8]{1,0:T(1,128)} copy(f32[1,8]{1,0:T(1,128)} %get-tuple-element.36) | data formatting | bytes 64
  104.3 1.4 %copy.38 = f32[1,16,512]{2,1,0:T(8,128)} copy(f32[1,16,512]{2,1,0:T(8,128)} %bitcast.29) | data formatting | bytes 65536
  105.7 1.3 %copy.39 = f32[1,8,512]{2,1,0:T(8,128)} copy(f32[1,8,512]{2,1,0:T(8,128)} %bitcast.30) | data formatting | bytes 32768
  107.0 1.2 %copy.40 = f32[1,8]{1,0:T(1,128)} copy(f32[1,8]{1,0:T(1,128)} %get-tuple-element.39) | data formatting | bytes 64

commit v3 on v2

--- a/solution.py
+++ b/solution.py
@@ -31,9 +31,24 @@
     return jnp.mean(x, axis=-1, keepdims=True)
 
 
+def far_first(size):
+    return sorted(range(size), key=lambda k: -min(k, size - k))
+
+
 def one_hot(rows, index):
     places = lax.broadcasted_iota(jnp.int32, (rows, index.shape[1]), 0)
     return jnp.where(places == index, 1.0, 0.0).astype(BF16)
+
+
+def interleaved(pair):
+    half = pair.shape[1]
+    spot = lax.broadcasted_iota(jnp.int32, (half, 2 * half), 1)
+    row = 2 * lax.broadcasted_iota(jnp.int32, (half, 2 * half), 0)
+    even = jnp.where(spot == row, 1.0, 0.0).astype(BF16)
+    odd = jnp.where(spot == row + 1, 1.0, 0.0).astype(BF16)
+    pair = pair.astype(BF16)
+    both = dot(pair[0:1], even) + dot(pair[1:2], odd)
+    return (both + 0.5).astype(jnp.int32)
 
 
 def mlp_forward(pre, outer):
@@ -56,8 +71,10 @@
 
 def layer_kernel(
     dims,
-    h_ref, e_ref, ncot_ref, ecot_ref, ew1, ew2, egain, nw1, nw2, ngain, src_ref, dst_ref, count_ref, out_ref,
+    h_ref, e_ref, ncot_hbm, ecot_hbm, ew1_hbm, ew2_hbm, egain, nw1_hbm, nw2_hbm, ngain,
+    src_ref, dst_ref, count_ref, out_ref,
     node_out, edge_out, w1e, w2e, ge, w1n, w2n, gn,
+    ew1, ew2, nw1, nw2, sem_in,
     rows_f32, send_a, recv_a, send_b, recv_b, node_in, edge_in,
     terms, from_core, chip_sum, from_y, y_sum, from_z,
     sem_a, sem_b, sem_down, sem_up,
@@ -101,19 +118,21 @@
         own = pltpu.make_async_copy(send.at[dom], recv.at[dom], sem.at[1])
         own.start()
 
-        def go(k, carry):
-            target = lax.rem(dom + k, count)
-            pltpu.make_async_remote_copy(
-                src_ref=send.at[target],
-                dst_ref=recv.at[dom],
-                send_sem=sem.at[0],
-                recv_sem=sem.at[1],
-                device_id={"dom": target},
-                device_id_type=MESH,
-            ).start()
-            return carry
-
-        lax.fori_loop(1, count, go, 0)
+        for dz in far_first(nz):
+            for dy in far_first(ny):
+                for dc in (1, 0):
+                    if dz + dy + dc > 0:
+                        target = (
+                            lax.rem(y + dy, ny) * nz + lax.rem(z + dz, nz)
+                        ) * 2 + lax.rem(core + dc, 2)
+                        pltpu.make_async_remote_copy(
+                            src_ref=send.at[target],
+                            dst_ref=recv.at[dom],
+                            send_sem=sem.at[0],
+                            recv_sem=sem.at[1],
+                            device_id={"dom": target},
+                            device_id_type=MESH,
+                        ).start()
 
     def arrived(recv, sem):
         pltpu.make_async_copy(recv, recv, sem.at[1]).wait()
@@ -125,15 +144,35 @@
         part = send.at[pl.ds(0, count - 1)]
         pltpu.make_async_copy(part, part, sem.at[0]).wait()
 
+    loads = [
+        pltpu.make_async_copy(source, target, sem_in.at[i])
+        for i, (source, target) in enumerate(
+            [(ew1_hbm, ew1), (ew2_hbm, ew2), (nw1_hbm, nw1), (nw2_hbm, nw2)]
+        )
+    ]
+    for load in loads:
+        load.start()
+    cot_loads = [
+        pltpu.make_async_copy(ncot_hbm, node_in, sem_in.at[4]),
+        pltpu.make_async_copy(ecot_hbm, edge_in, sem_in.at[5]),
+    ]
+
+    @pl.when(pipe == phases - 1)
+    def _():
+        for load in cot_loads:
+            load.start()
+
     h = h_ref[...]
     e = e_ref[...]
-    to_send = one_hot(nodes, out_ref[...])
+    to_send = one_hot(nodes, interleaved(out_ref[...].astype(F32)))
     by_dst = one_hot(nodes, dst_ref[...])
     by_src = one_hot(nodes + 2 * count, src_ref[...])
     spread(contract(to_send, h), send_a)
     pl.semaphore_wait(barrier, count + 1)
     exchange(send_a, recv_a, sem_a)
 
+    for load in loads:
+        load.wait()
     live = jnp.where(
         lax.broadcasted_iota(jnp.int32, (edges, width), 0) < count_ref[...], 1.0, 0.0
     )
@@ -163,8 +202,8 @@
 
     @pl.when(pipe == phases - 1)
     def _():
-        node_in[...] = ncot_ref[...]
-        edge_in[...] = ecot_ref[...]
+        for load in cot_loads:
+            load.wait()
 
     @pl.when(pipe < phases - 1)
     def _():
@@ -227,7 +266,7 @@
             [n2[b2 * d : b2 * d + b2], gain_rows], axis=0
         ).astype(BF16)
 
-    order = sorted(range(nz), key=lambda k: -min(k, nz - k))
+    order = far_first(nz)
     places = [lax.rem(z + k, nz) for k in order]
     core_copies, y_copies, z_copies = [], [], []
     for i, place in enumerate(places):
@@ -310,6 +349,12 @@
         copy.wait_send()
 
 
+def handed_on(*refs):
+    half = len(refs) // 2
+    for source, target in zip(refs[:half], refs[half:]):
+        target[...] = source[...]
+
+
 def on_device(
     node_states, edge_states, node_cot, edge_cot,
     edge_w1, edge_w2, edge_gain, node_w1, node_w2, node_gain,
@@ -325,12 +370,13 @@
     a1, a2, b1 = edge_w1.shape[1] // count, hid // count, node_w1.shape[1] // count
     rows = a1 + 2 * a2 + b1 + 8
     vmem = pl.BlockSpec(memory_space=pltpu.VMEM)
+    hbm = pl.BlockSpec(memory_space=pl.ANY)
     dma = pltpu.SemaphoreType.DMA
 
     def shape(*sizes, kind=F32):
         return jax.ShapeDtypeStruct(sizes, kind)
 
-    node_out, edge_out, w1e, w2e, ge, w1n, w2n, gn = pl.pallas_call(
+    results = pl.pallas_call(
         functools.partial(layer_kernel, (phases, ny, nz)),
         out_shape=(
             shape(nodes, width, kind=BF16),
@@ -342,9 +388,14 @@
             shape(a2, width),
             shape(1, width // count),
         ),
-        in_specs=[vmem] * 14,
+        in_specs=[vmem] * 2 + [hbm] * 4 + [vmem] + [hbm] * 2 + [vmem] * 5,
         out_specs=[vmem] * 8,
         scratch_shapes=[
+            pltpu.VMEM(edge_w1.shape[1:], BF16),
+            pltpu.VMEM(edge_w2.shape[1:], BF16),
+            pltpu.VMEM(node_w1.shape[1:], BF16),
+            pltpu.VMEM(node_w2.shape[1:], BF16),
+            dma((6,)),
             pltpu.VMEM((2 * count, width), F32),
             pltpu.VMEM((count, 2, width), BF16),
             pltpu.VMEM((count, 2, width), BF16),
@@ -376,8 +427,15 @@
     )(
         node_states[0, 0], edge_states[0, 0], node_cot[0], edge_cot[0],
         edge_w1[0], edge_w2[0], edge_gain, node_w1[0], node_w2[0], node_gain,
-        edge_src[None], edge_dst[None], edge_count[None], send_rows.reshape(1, 2 * count),
-    )
+        edge_src[None], edge_dst[None], edge_count[None], send_rows[0].T,
+    )
+    node_out, edge_out, w1e, w2e, ge, w1n, w2n, gn = pl.pallas_call(
+        handed_on,
+        out_shape=tuple(jax.ShapeDtypeStruct(r.shape, r.dtype) for r in results),
+        in_specs=[vmem] * 8,
+        out_specs=[vmem] * 8,
+        name="results",
+    )(*results)
     return (
         node_out[None, None], edge_out[None, None],
         w1e[None], w2e[None], ge, w1n[None], w2n[None], gn,

time: 109 us -> 92.1 us (0.84)
  local copies, waits for them, and re-layouts: 12.4 us -> 0 us
  Pallas kernels: 94.5 us -> 90.7 us
    unnamed x9 -> x0, local copies, waits for them, and re-layouts: 11.7 us -> none
    pallas_call x1, Pallas kernels: 94.5 us -> 88.9 us  [on_device(): pl.pallas_call(functools.partial(layer_kernel, (phases, ny, nz)), out_sha...]
    pallas_call x0 -> x1, Pallas kernels: none -> 1.74 us  [on_device(): pl.pallas_call(handed_on, out_shape=tuple((jax.ShapeDtypeStruct(r.shape,...]
where the time goes in v3:
time: 92.1 us; the launch traced here: 92 us
  Pallas kernels  90.7 us (98%)
  between operations  1.29 us (1%)
    pallas_call x1, Pallas kernels, on_device(): pl.pallas_call(functools.partial(layer_kernel, (phases, ny, nz)), out_sha...  88.9 us

profile of v3, /device:TPU:32, one launch (start us, length us, event | category | flops | bytes accessed | tf_op | source)
XLA Modules:
  0.0 92.0 jit_solution(9698968909693003017)
XLA Ops:
  1.3 88.9 %relay_backward.1 = (bf16[64,512]{1,0:T(8,128)(2,1)}, bf16[256,512]{1,0:T(8,128)(2,1)}, f32[24,512]{1,0:T(8,128)}, f32[8,512]{1,0:T(8,128)}, f32[1,8]{1,0:T(1,12...) custom-call(bf16[64,512]{1,0:T(8,128)(2,1)} %bitcast.27, bf16[256,512]{1,0:T(8,128)(2,1)} %bitcast.25, ...), custom_call_target="tpu_custom_call" | custom-call | tf_op jit(solution)/shard_map/relay_backward/pallas_call | solution.py:379
  90.2 1.7 %results.1 = (bf16[64,512]{1,0:T(8,128)(2,1)}, bf16[256,512]{1,0:T(8,128)(2,1)}, f32[24,512]{1,0:T(8,128)}, f32[8,512]{1,0:T(8,128)}, f32[1,8]{1,0:T(1,128)}, /*...) custom-call(bf16[64,512]{1,0:T(8,128)(2,1)} %get-tuple-element.24.refs_0_, ...), custom_call_target="tpu_custom_call" | custom-call | tf_op jit(solution)/shard_map/results/pallas_call | solution.py:432
